TPU v7x, 512 devices: a whole 4x8x8 slice. The times are simulated.
512 devices in a mesh: lat: 16 (over y, core), lev: 32 (over z, x).
Axes of the slice: x: 4, y: 8, z: 8, core: 2. Of those that a mesh axis runs over, the one named last changes fastest.
Arguments:
- fields: float32 [4, 128, 128, 1152], P(None, 'lev', 'lat'), may hold values from -6 to 6
- winds: float32 [2, 128, 128, 1152], P(None, 'lev', 'lat'), may hold values from -0.3 to 0.3
- remap_weight: bfloat16 [128, 128], replicated, may hold values from -0.5 to 0.5
- w_first: bfloat16 [512, 512], replicated, may hold values from -0.25 to 0.25
- w_second: bfloat16 [512, 512], replicated, may hold values from -0.25 to 0.25
- w_third: bfloat16 [512, 512], replicated, may hold values from -0.25 to 0.25
- lon_counts: int32 [16, 32], P('lat'), may hold values from 1 to 128, 1152 in all within a row
- group_list: int32 [16, 6], replicated, may hold values from 0 to 127, as said below
Outputs:
- columns_out: bfloat16 [4, 128, 128, 4096], P(None, None, 'lat', 'lev')
Inputs may be any that keep to these rules, and one draw needn't show every extreme that they name: `lon_counts`: each row sums to 1152, and its largest entry is exactly 128. `group_list`: row p lists in ascending order the 6 latitude rows whose columns owner p (index p of lat) processes; no row appears twice; every row j with j // 8 equal to 8 appears; at most 1 row of one owner's list have the same j // 8, and some owner has exactly 1 such rows.
All inputs are finite; a program needn't handle non-finite values.
Results may differ from a plain program's by a relative error of at most 0.0053.
Values may be sent and summed in bfloat16 or wider, within the bound.
A program may use at most 64 MiB of HBM per device.

v0:
```python
import jax
import jax.numpy as jnp
from jax import lax
from jax.sharding import PartitionSpec as P

DIFFUSION = 0.15


def padded(x, sides, width):
    for axis, dim in sides:
        size, length = (lax.axis_size(axis), x.shape[dim])
        up = [(i, (i + 1) % size) for i in range(size - 1)]
        down = [(j, i) for i, j in up]
        last = lax.slice_in_dim(x, length - width, length, axis=dim)
        first = lax.slice_in_dim(x, 0, width, axis=dim)
        before = lax.ppermute(last, axis, up)
        after = lax.ppermute(first, axis, down)
        x = jnp.concatenate([before, x, after], axis=dim)
    return x


def flux_divergence(values, east_wind, north_wind, first_row, total_rows):
    inner_count = values.shape[-2] - 2
    face_flux = (
        0.25
        * (north_wind[..., :-1, :] + north_wind[..., 1:, :])
        * (values[..., :-1, :] + values[..., 1:, :])
    )
    face_flux = face_flux - DIFFUSION * (values[..., 1:, :] - values[..., :-1, :])
    faces = first_row + jnp.arange(inner_count + 1, dtype=jnp.int32)
    keep_face = ((faces >= 1) & (faces <= total_rows - 1)).astype(jnp.float32)[:, None]
    face_flux = face_flux * keep_face
    inner = values[..., 1:-1, :]
    inner_wind = east_wind[..., 1:-1, :]
    west_values = jnp.roll(inner, 1, axis=-1)
    west_wind = jnp.roll(inner_wind, 1, axis=-1)
    side_flux = 0.25 * (west_wind + inner_wind) * (west_values + inner) - DIFFUSION * (
        inner - west_values
    )
    return -(face_flux[..., 1:, :] - face_flux[..., :-1, :]) - (
        jnp.roll(side_flux, -1, axis=-1) - side_flux
    )


def convect(columns, w_first, w_second, w_third):
    pattern = (((0,), (0,)), ((), ()))
    hidden_one = jax.nn.silu(
        lax.dot_general(w_first, columns, pattern, preferred_element_type=jnp.float32)
    ).astype(jnp.bfloat16)
    hidden_two = jax.nn.silu(
        lax.dot_general(w_second, hidden_one, pattern, preferred_element_type=jnp.float32)
    ).astype(jnp.bfloat16)
    return lax.dot_general(w_third, hidden_two, pattern, preferred_element_type=jnp.float32).astype(
        jnp.bfloat16
    )


def shards(fields, winds, remap_weight, w_first, w_second, w_third, lon_counts, group_list):
    field_count, level_count, lat_rows, lon_total = fields.shape
    band_count = lax.axis_size("lat")
    band_index = lax.axis_index("lat")
    owner_count = lax.axis_size("lev")
    first_row = band_index * lat_rows
    total_rows = band_count * lat_rows
    stacked = jnp.concatenate([fields, winds], axis=0)
    extended = padded(stacked, (("lat", 2),), 1)
    east_wind = extended[field_count]
    north_wind = extended[field_count + 1]
    predicted = fields + flux_divergence(
        extended[:field_count], east_wind, north_wind, first_row, total_rows
    )
    widened = padded(predicted, (("lat", 2),), 1)
    second = flux_divergence(widened, east_wind, north_wind, first_row, total_rows)
    advected = 0.5 * (fields + predicted + second)
    lon_split = lon_counts[0]
    lon_start = jnp.cumsum(lon_split) - lon_split
    slot_width = 128 * ((2 * lon_total // owner_count + 127) // 128)
    offsets = jnp.arange(slot_width, dtype=jnp.int32)
    lon_index = (lon_start[:, None] + offsets[None, :]).reshape(-1)
    in_range = (offsets[None, :] < lon_split[:, None]).reshape(-1)
    selector = (
        (jnp.arange(lon_total, dtype=jnp.int32)[:, None] == lon_index[None, :]) & in_range[None, :]
    ).astype(jnp.bfloat16)
    packed = jnp.dot(
        advected.astype(jnp.bfloat16).reshape(-1, lon_total),
        selector,
        preferred_element_type=jnp.float32,
    )
    packed = packed.astype(jnp.bfloat16).reshape(
        field_count, level_count, lat_rows, owner_count * slot_width
    )
    block = lax.all_to_all(packed, "lev", split_axis=3, concat_axis=1, tiled=True)
    count_f, count_m, count_r, count_c = block.shape
    mixed = jnp.stack(
        [
            jnp.dot(
                remap_weight,
                block[index].reshape(count_m, count_r * count_c),
                preferred_element_type=jnp.float32,
            )
            for index in range(count_f)
        ]
    )
    remapped = block.astype(jnp.float32) + mixed.reshape(count_f, count_m, count_r, count_c)
    features = remapped.astype(jnp.bfloat16).reshape(-1, lat_rows, slot_width)
    feature_count = features.shape[0]
    local_hits = jnp.any(
        group_list[:, :, None]
        == (first_row + jnp.arange(lat_rows, dtype=jnp.int32))[None, None, :],
        axis=(0, 1),
    )
    tendency = convect(
        features.reshape(feature_count, lat_rows * slot_width), w_first, w_second, w_third
    ).reshape(feature_count, lat_rows, slot_width)
    tendency = jnp.where(local_hits[None, :, None], tendency, jnp.zeros_like(tendency))
    columns_out = remapped + tendency.reshape(field_count, -1, lat_rows, slot_width).astype(
        jnp.float32
    )
    return columns_out.astype(jnp.bfloat16)


def solution(mesh):
    in_specs = (
        P(None, "lev", "lat", None),
        P(None, "lev", "lat", None),
        P(),
        P(),
        P(),
        P(),
        P("lat", None),
        P(),
    )
    out_specs = P(None, None, "lat", "lev")
    return jax.shard_map(shards, mesh=mesh, in_specs=in_specs, out_specs=out_specs, check_vma=False)
```

profile of v0, /device:TPU:27, one launch (start us, length us, event | category | flops | bytes accessed | tf_op | source)
XLA Modules:
  0.0 171.7 jit_solution(3574603970590724768)
XLA Ops:
  0.0 0.0 copy-start
  0.0 1.2 constant_dynamic-update-slice_fusion.1
  1.2 1.0 constant_dynamic-update-slice_fusion
  2.2 0.1 fusion.51
  2.4 5.0 %collective-permute-start = (f32[6,4,1,1152]{3,0,2,1:T(8,128)S(1)}, f32[6,4,1,1152]{3,0,2,1:T(8,128)S(1)}, u32[]{:S(2)}, u32[]{:S(2)}) collective-permute-start(f32[6,4,1,1152]{3,0,2,1:T(8,128)S(1)} %copy.69), channel_id=1, source_target_pairs={{0,32},{32,64},{64,96},{96,128},{128,160},{160,192},{192,224},{224... | collective-permute-start | bytes 331784 | tf_op jit(solution)/shard_map/ppermute | solution.py:16
  7.4 1.9 %collective-permute-start.1 = (f32[6,4,1,1152]{3,0,2,1:T(8,128)S(1)}, f32[6,4,1,1152]{3,0,2,1:T(8,128)S(1)}, u32[]{:S(2)}, u32[]{:S(2)}) collective-permute-start(f32[6,4,1,1152]{3,0,2,1:T(8,128)S(1)} %copy.70), channel_id=1, source_target_pairs={{32,0},{64,32},{96,64},{128,96},{160,128},{192,160},{224,192},{256... | collective-permute-start | bytes 331784 | tf_op jit(solution)/shard_map/ppermute | solution.py:17
  9.3 0.0 copy-done.1
  9.3 0.1 slice.138
  9.4 0.1 fusion.48
  9.5 0.1 copy.83
  9.6 0.1 reduce-window.8
  9.6 0.1 reduce
  9.8 0.1 add_bitcast_fusion
  9.8 0.0 collective-permute-done
  9.8 0.1 copy.71
  10.0 5.1 %collective-permute-done.1 = f32[6,4,1,1152]{3,0,2,1:T(8,128)S(1)} collective-permute-done((f32[6,4,1,1152]{3,0,2,1:T(8,128)S(1)}, f32[6,4,1,1152]{3,0,2,1:T(8,128)S(1)}, u32[]{:S(2)}, u32[]{:S(2)}) %collective-permute-start.1) | collective-permute-done | bytes 110624 | tf_op jit(solution)/shard_map/ppermute | solution.py:17
  15.1 0.1 copy.72
  15.2 0.1 pad_maximum_fusion.6
  15.3 0.1 copy_bitcast_fusion
  15.4 0.1 slice.160
  15.5 0.1 fusion.47
  15.7 0.2 multiply_subtract_fusion.1
  15.9 0.2 slice.163
  16.2 0.4 subtract_multiply_fusion
  16.6 0.2 fusion.33
  16.9 0.1 slice.169
  16.9 0.1 fusion.52
  17.1 1.9 %collective-permute-start.2 = (f32[4,4,1,1152]{3,1,2,0:T(4,128)S(1)}, f32[4,4,1,1152]{3,1,2,0:T(4,128)S(1)}, u32[]{:S(2)}, u32[]{:S(2)}) collective-permute-start(f32[4,4,1,1152]{3,1,2,0:T(4,128)S(1)} %copy.79), channel_id=1, source_target_pairs={{0,32},{32,64},{64,96},{96,128},{128,160},{160,192},{192,224},{224... | collective-permute-start | bytes 221192 | tf_op jit(solution)/shard_map/ppermute | solution.py:16
  19.0 2.4 %collective-permute-start.3 = (f32[4,4,1,1152]{3,1,2,0:T(4,128)S(1)}, f32[4,4,1,1152]{3,1,2,0:T(4,128)S(1)}, u32[]{:S(2)}, u32[]{:S(2)}) collective-permute-start(f32[4,4,1,1152]{3,1,2,0:T(4,128)S(1)} %copy.81), channel_id=1, source_target_pairs={{32,0},{64,32},{96,64},{128,96},{160,128},{192,160},{224,192},{256... | collective-permute-start | bytes 221192 | tf_op jit(solution)/shard_map/ppermute | solution.py:17
  21.4 0.2 multiply_subtract_fusion
  21.7 0.2 slice.171
  21.9 0.0 collective-permute-done.2
  21.9 0.1 copy.80
  22.0 3.9 %collective-permute-done.3 = f32[4,4,1,1152]{3,1,2,0:T(4,128)S(1)} collective-permute-done((f32[4,4,1,1152]{3,1,2,0:T(4,128)S(1)}, f32[4,4,1,1152]{3,1,2,0:T(4,128)S(1)}, u32[]{:S(2)}, u32[]{:S(2)}) %collective-permute-start.3) | collective-permute-done | bytes 73760 | tf_op jit(solution)/shard_map/ppermute | solution.py:17
  25.9 0.1 copy.82
  26.0 0.4 fusion.22
  26.4 0.2 fusion.30
  26.6 4.8 %fusion.5 = bf16[128,4096]{1,0:T(8,128)(2,1)S(1)} fusion(bf16[128,1152]{1,0:T(8,128)(2,1)S(1)} %bitcast.123, s32[4096]{0:T(1024)S(1)} %add_bitcast_fusion, pred[4096]{0:T(1024)(128)(4,1)S(1)} %fusion.48), kind=kOutput, calls=%fused_computation.5 | convolution fusion | flops 1217921024 | bytes 1363968 | tf_op jit(solution)/shard_map/dot_general | solution.py:84
  31.5 17.0 %copy.84 = bf16[4,4,8,4096]{2,1,0,3:T(4,128)(2,1)} copy(bf16[4,4,8,4096]{3,2,1,0:T(8,128)(2,1)S(1)} %bitcast.118) | data formatting | bytes 2097152 | tf_op jit(solution)/shard_map/reshape | solution.py:89
  48.5 20.6 %reshape.119 = bf16[32,2,8192]{2,1,0:T(2,128)(2,1)} reshape(bf16[4096,4,4,8]{3,2,1,0:T(4,128)(2,1)} %bitcast.106) | data formatting | bytes 2097152
  69.1 13.0 %all-to-all-start = ((bf16[32,2,8192]{2,1,0:T(2,128)(2,1)}), bf16[32,2,8192]{2,1,0:T(2,128)(2,1)S(1)}, u32[]{:S(2)}, u32[]{:S(2)}) async-start(bf16[32,2,8192]{2,1,0:T(2,128)(2,1)} %reshape.119), calls=%async_computation | async-start | bytes 2097152 | tf_op jit(solution)/shard_map/all_to_all | solution.py:92
  82.2 0.0 copy-done.4
  82.2 0.2 compare_reduce_fusion
  82.4 26.6 %all-to-all-done = bf16[32,2,8192]{2,1,0:T(2,128)(2,1)S(1)} async-done(((bf16[32,2,8192]{2,1,0:T(2,128)(2,1)}), bf16[32,2,8192]{2,1,0:T(2,128)(2,1)S(1)}, u32[]{:S(2)}, u32[]{:S(2)}) %all-to-all-start) | async-done | bytes 1048608 | tf_op jit(solution)/shard_map/all_to_all | solution.py:92
  109.0 20.8 %reshape.120 = bf16[4096,4,4,8]{3,2,1,0:T(4,128)(2,1)} reshape(bf16[32,2,8192]{2,1,0:T(2,128)(2,1)S(1)} %all-to-all-done) | data formatting | bytes 2097152
  129.8 19.2 %copy.85 = bf16[4,4,8,32,128]{4,2,1,3,0:T(8,128)(2,1)S(1)} copy(bf16[4,4,8,32,128]{2,1,0,4,3:T(4,128)(2,1)} %bitcast.107) | data formatting | bytes 2097152 | tf_op jit(solution)/shard_map/all_to_all | solution.py:92
  149.0 0.0 copy-start.3
  149.0 1.6 bitcast_convert_fusion
  150.7 0.1 fusion.50
  150.8 0.3 fusion.37
  151.0 0.2 copy.88
  151.3 0.3 fusion.43
  151.5 1.0 copy.86
  152.5 0.2 fusion.40
  152.8 1.0 copy.87
  153.8 0.2 fusion.34
  154.1 1.0 copy.89
  155.1 1.6 pad_maximum_fusion
  156.7 0.4 copy-done.2
  157.1 2.5 %fusion.15 = bf16[512,1024]{0,1:T(8,128)(2,1)} fusion(bf16[512,512]{1,0:T(8,128)(2,1)S(1)} %copy-done, f32[64,8,8,128]{3,2,1,0:T(8,128)S(1)} %bitcast.113, f32[64,8,8,128]{3,2,1,0:T(8,128)S(1)} %bitcast.111), kind=kOutput, calls=%fused_computation.20 | convolution fusion | flops 540540928 | bytes 5767168 | tf_op jit(solution)/shard_map/dot_general | solution.py:48
  159.7 3.9 %fusion.17 = bf16[512,1024]{0,1:T(8,128)(2,1)} fusion(bf16[512,512]{1,0:T(8,128)(2,1)} %param.13, bf16[512,1024]{0,1:T(8,128)(2,1)} %fusion.15, bf16[512,512]{1,0:T(8,128)(2,1)} %param.12), kind=kOutput, calls=%fused_computation.23 | convolution fusion | flops 1076887552 | bytes 3145728 | tf_op jit(solution)/shard_map/dot_general | solution.py:53
  163.5 2.1 %reshape.115 = bf16[4,128,8,128]{1,0,3,2:T(4,128)(2,1)} reshape(bf16[512,1024]{0,1:T(8,128)(2,1)} %fusion.17) | data formatting | bytes 2097152 | tf_op jit(solution)/shard_map/reshape | solution.py:114
  165.7 2.9 %copy.90 = bf16[4,128,8,128]{3,2,1,0:T(8,128)(2,1)} copy(bf16[4,128,8,128]{1,0,3,2:T(4,128)(2,1)} %reshape.115) | data formatting | bytes 2097152 | tf_op jit(solution)/shard_map/reshape | solution.py:114
  168.6 3.0 %add_convert_fusion = bf16[4,128,8,128]{3,2,1,0:T(8,128)(2,1)} fusion(f32[4,128,8,128]{3,2,1,0:T(8,128)S(1)} %bitcast.112, bf16[4,128,8,128]{3,2,1,0:T(8,128)(2,1)} %copy.90, pred[8]{0:T(512)(128)(4,1)S(1)} %compare_reduce_fusion, f32[1,128,8,128]{3,2,1,0:T(8,128)} %copy.89, f32[1,128,8,128]{3,2,1,0:T(8,128)S(1)} %copy.88, f32[1,128,8,128]{3,2,1,0:T(8,128)} %copy.87, ...), kind=kLoop, calls=%fused_computation.19 | loop fusion | flops 4194304 | bytes 6291464 | tf_op jit(solution)/shard_map/convert_element_type | solution.py:119
  (20 shorter events, 0.2 us)
Async XLA Ops:
  0.0 156.7 %copy-start = (bf16[512,512]{1,0:T(8,128)(2,1)S(1)}, bf16[512,512]{1,0:T(8,128)(2,1)}, u32[]{:S(2)}) copy-start(bf16[512,512]{1,0:T(8,128)(2,1)} %param.11) | copy-start | bytes 1572868
  0.0 9.3 %copy-start.1 = (f32[4,4,8,1152]{3,2,1,0:T(8,128)S(1)}, f32[4,4,8,1152]{3,2,1,0:T(8,128)}, u32[]{:S(2)}) copy-start(f32[4,4,8,1152]{3,2,1,0:T(8,128)} %param.8) | copy-start | bytes 1769476
  0.0 9.4 %copy-start.5 = (s32[1,32]{1,0:T(1,128)S(1)}, s32[1,32]{1,0:T(1,128)}, u32[]{:S(2)}) copy-start(s32[1,32]{1,0:T(1,128)} %param.14) | copy-start | bytes 388
  2.4 7.5 %collective-permute-start = (f32[6,4,1,1152]{3,0,2,1:T(8,128)S(1)}, f32[6,4,1,1152]{3,0,2,1:T(8,128)S(1)}, u32[]{:S(2)}, u32[]{:S(2)}) collective-permute-start(f32[6,4,1,1152]{3,0,2,1:T(8,128)S(1)} %copy.69), channel_id=1, source_target_pairs={{0,32},{32,64},{64,96},{96,128},{128,160},{160,192},{192,224},{224... | collective-permute-start | bytes 331784 | tf_op jit(solution)/shard_map/ppermute | solution.py:16
  7.4 7.7 %collective-permute-start.1 = (f32[6,4,1,1152]{3,0,2,1:T(8,128)S(1)}, f32[6,4,1,1152]{3,0,2,1:T(8,128)S(1)}, u32[]{:S(2)}, u32[]{:S(2)}) collective-permute-start(f32[6,4,1,1152]{3,0,2,1:T(8,128)S(1)} %copy.70), channel_id=1, source_target_pairs={{32,0},{64,32},{96,64},{128,96},{160,128},{192,160},{224,192},{256... | collective-permute-start | bytes 331784 | tf_op jit(solution)/shard_map/ppermute | solution.py:17
  17.1 4.8 %collective-permute-start.2 = (f32[4,4,1,1152]{3,1,2,0:T(4,128)S(1)}, f32[4,4,1,1152]{3,1,2,0:T(4,128)S(1)}, u32[]{:S(2)}, u32[]{:S(2)}) collective-permute-start(f32[4,4,1,1152]{3,1,2,0:T(4,128)S(1)} %copy.79), channel_id=1, source_target_pairs={{0,32},{32,64},{64,96},{96,128},{128,160},{160,192},{192,224},{224... | collective-permute-start | bytes 221192 | tf_op jit(solution)/shard_map/ppermute | solution.py:16
  19.0 6.9 %collective-permute-start.3 = (f32[4,4,1,1152]{3,1,2,0:T(4,128)S(1)}, f32[4,4,1,1152]{3,1,2,0:T(4,128)S(1)}, u32[]{:S(2)}, u32[]{:S(2)}) collective-permute-start(f32[4,4,1,1152]{3,1,2,0:T(4,128)S(1)} %copy.81), channel_id=1, source_target_pairs={{32,0},{64,32},{96,64},{128,96},{160,128},{192,160},{224,192},{256... | collective-permute-start | bytes 221192 | tf_op jit(solution)/shard_map/ppermute | solution.py:17
  69.1 13.1 %copy-start.4 = (s32[16,6]{0,1:T(8,128)S(1)}, s32[16,6]{0,1:T(8,128)}, u32[]{:S(2)}) copy-start(s32[16,6]{0,1:T(8,128)} %param.15) | copy-start | bytes 1156
  69.1 39.9 %all-to-all-start = ((bf16[32,2,8192]{2,1,0:T(2,128)(2,1)}), bf16[32,2,8192]{2,1,0:T(2,128)(2,1)S(1)}, u32[]{:S(2)}, u32[]{:S(2)}) async-start(bf16[32,2,8192]{2,1,0:T(2,128)(2,1)} %reshape.119), calls=%async_computation | async-start | bytes 2097152 | tf_op jit(solution)/shard_map/all_to_all | solution.py:92
  149.0 1.7 %copy-start.3 = (bf16[128,128]{1,0:T(8,128)(2,1)S(1)}, bf16[128,128]{1,0:T(8,128)(2,1)}, u32[]{:S(2)}) copy-start(bf16[128,128]{1,0:T(8,128)(2,1)} %param.10) | copy-start | bytes 98308
  155.1 2.1 %copy-start.2 = (f32[4,32,4,8,128]{4,3,2,1,0:T(8,128)S(1)}, f32[4,32,4,8,128]{4,3,2,1,0:T(8,128)}, u32[]{:S(2)}) copy-start(f32[4,32,4,8,128]{4,3,2,1,0:T(8,128)} %bitcast_convert_fusion) | copy-start | bytes 6291460
where the time goes:
time: 173 us; the launch traced here: 172 us
  local copies, waits for them, and re-layouts  90.3 us (52%)
  waiting for transfers between devices  35.6 us (21%)
  starting transfers between devices  24.3 us (14%)
  matrix products  12.2 us (7%)
  other arithmetic  8.83 us (5%)
    unnamed x15, local copies, waits for them, and re-layouts  43 us
    all_to_all x1, waiting for transfers between devices, shards(): lax.all_to_all(packed, 'lev', split_axis=3, concat_axis=1, tiled=True)  26.6 us
    all_to_all x1, local copies, waits for them, and re-layouts, shards(): lax.all_to_all(packed, 'lev', split_axis=3, concat_axis=1, tiled=True)  19.2 us
    reshape x1, local copies, waits for them, and re-layouts, shards(): packed.astype(jnp.bfloat16)  17 us
    all_to_all x1, starting transfers between devices, shards(): lax.all_to_all(packed, 'lev', split_axis=3, concat_axis=1, tiled=True)  13 us
    ppermute x2, waiting for transfers between devices, padded(): after = lax.ppermute(first, axis, down)  9 us
    ppermute x2, starting transfers between devices, padded(): before = lax.ppermute(last, axis, up)  6.9 us
    reshape x2, local copies, waits for them, and re-layouts, shards(): tendency = convect(features.reshape(feature_count, lat_rows * slot_width)...  5.06 us
  transfers between devices with their start and end apart: 5, of which 3 were waited for; matrix products, arithmetic and copies ran while one was open for 1% of the time, Pallas kernels for 0%

commit v1 on v0

v1 whole, which is shorter than its diff:
```python
import functools

import jax
import jax.numpy as jnp
from jax import lax
from jax.experimental import pallas as pl
from jax.experimental.pallas import tpu as pltpu
from jax.sharding import PartitionSpec as P

DIFFUSION = 0.15
SLOT = 128
MESH = pl.DeviceIdType.MESH
BF = jnp.bfloat16
F32 = jnp.float32


def kernel(
    n_lat, n_lev, x_size, lev_total,
    cnt_ref, grp_ref, fields_hbm, winds_hbm, rw_hbm, w1_hbm, w2_hbm, w3_hbm,
    out_ref,
    up_buf, down_buf, lo_buf, hi_buf,
    tracer, wind_in, sown, ew, nw, ah, bh, ag, bg, pred, adv,
    send, recv,
    rw_in, w1_in, w2_in, w3_in, mix, w1t, w2t, w3t, done,
    halo_send, halo_recv, send_sem, recv_sem, load_sem, in_sem,
):
    rows, fields_count = 8, 4
    group = send.shape[2]
    levels = group // fields_count
    halves = group // 8
    lon = fields_hbm.shape[1]
    feats = n_lev * group
    chunks = ((2, 3), (4, 5), (0, 1), (6, 7))

    lat = lax.axis_index("lat")
    me = lax.axis_index("lev")
    up, down = lax.rem(lat + 1, n_lat), lax.rem(lat + n_lat - 1, n_lat)
    z_size = n_lev // x_size
    my_z, my_x = me // x_size, lax.rem(me, x_size)

    def peer_of(i):
        step, dx = i // x_size, lax.rem(i, x_size) + 1
        dz = z_size // 2 + (1 - 2 * lax.rem(step, 2)) * ((step + 1) // 2)
        return lax.rem(my_z + dz, z_size) * x_size + lax.rem(my_x + dx, x_size)

    barrier = pltpu.get_barrier_semaphore()
    for other in (up, down):
        pl.semaphore_signal(barrier, inc=1, device_id={"lat": other}, device_id_type=MESH)

    @pl.loop(0, n_lev - 1)
    def _(i):
        pl.semaphore_signal(barrier, inc=1, device_id={"lev": peer_of(i)}, device_id_type=MESH)

    tiles = lon // SLOT
    columns = [slice(t * SLOT, (t + 1) * SLOT) for t in range(tiles)]
    inputs = []
    for t, part in enumerate(columns):
        cut = pl.ds(t * SLOT, SLOT)
        inputs.append(pltpu.make_async_copy(fields_hbm.at[:, cut], tracer.at[t], in_sem.at[0, t]))
        inputs.append(pltpu.make_async_copy(winds_hbm.at[:, cut], wind_in.at[t], in_sem.at[1, t]))
    for copy in inputs:
        copy.start()

    loads = [
        pltpu.make_async_copy(src, dst, load_sem.at[i])
        for i, (src, dst) in enumerate(
            ((rw_hbm, rw_in), (w1_hbm, w1_in), (w2_hbm, w2_in), (w3_hbm, w3_in))
        )
    ]
    for load in loads:
        load.start()

    def twice(x):
        return jnp.concatenate([x, x], axis=0)

    for t, part in enumerate(columns):
        inputs[2 * t].wait()
        inputs[2 * t + 1].wait()
        for r in range(rows):
            for h in range(halves):
                sown[r, h, :, part] = tracer[t, pl.ds(h * 8 * rows + r, 8, stride=rows), :]
            for which, kept in ((0, ew), (1, nw)):
                kept[r, :, part] = twice(wind_in[t, pl.ds(which * levels * rows + r, levels, stride=rows), :])
    for buf, far, near, order in ((up_buf, 6, 7, (6, 7)), (down_buf, 1, 0, (0, 1))):
        for k, r in enumerate(order):
            for h in range(halves):
                buf[k * halves + h] = sown[r, h]
        buf[2 * halves] = jnp.concatenate([ew[near, :levels], nw[near, :levels]], axis=0)
        buf[2 * halves + 1] = nw[far]

    def value(r, h):
        if r < 0:
            return lo_buf[(r + 2) * halves + h]
        if r >= rows:
            return hi_buf[(r - rows) * halves + h]
        return sown[r, h]

    def east(r):
        if r < 0:
            return twice(lo_buf[2 * halves, :levels])
        if r >= rows:
            return twice(hi_buf[2 * halves, :levels])
        return ew[r]

    def north(r):
        if r == -2:
            return lo_buf[2 * halves + 1]
        if r == -1:
            return twice(lo_buf[2 * halves, levels:])
        if r == rows:
            return twice(hi_buf[2 * halves, levels:])
        if r == rows + 1:
            return hi_buf[2 * halves + 1]
        return nw[r]

    def make_side(r):
        u = east(r)
        c = 0.25 * (pltpu.roll(u, 1, axis=1) + u)
        ah[r + 1] = c + DIFFUSION
        bh[r + 1] = c - DIFFUSION

    def make_face(j):
        c = 0.25 * (north(j - 1) + north(j))
        a, b = c + DIFFUSION, c - DIFFUSION
        if j == 0:
            keep = jnp.where(lat > 0, 1.0, 0.0).astype(F32)
            a, b = a * keep, b * keep
        if j == rows:
            keep = jnp.where(lat < n_lat - 1, 1.0, 0.0).astype(F32)
            a, b = a * keep, b * keep
        ag[j + 1] = a
        bg[j + 1] = b

    def sweep(get, span, emit):
        for h in range(halves):
            face = None
            for r in span:
                here = get(r, h)
                if face is None:
                    face = ag[r + 1] * get(r - 1, h) + bg[r + 1] * here
                after = ag[r + 2] * here + bg[r + 2] * get(r + 1, h)
                side = ah[r + 1] * pltpu.roll(here, 1, axis=1) + bh[r + 1] * here
                change = (face - after) + (side - pltpu.roll(side, lon - 1, axis=1))
                emit(r, h, here, change)
                face = after

    def first_step(r, h, here, change):
        pred[r + 1, h] = here + change

    def second_step(r, h, here, change):
        result = 0.5 * (value(r, h) + here + change)
        for t, part in enumerate(columns):
            adv[t, r, h] = result[:, part]

    def guess(r, h):
        return pred[r + 1, h]

    lane = lax.broadcasted_iota(jnp.int32, (8, SLOT), 1)

    def compact(c):
        def body(k, start):
            tile = start >> 7
            shift = start & (SLOT - 1)
            back = (SLOT - shift) & (SLOT - 1)
            take = lane < SLOT - shift
            for i, r in enumerate(chunks[c]):
                parts = []
                for h in range(halves):
                    a = pltpu.roll(adv[tile, r, h], back, axis=1)
                    b = pltpu.roll(adv[tile + 1, r, h], back, axis=1)
                    parts.append(jnp.where(take, a, b))
                send[c, k, :, i * SLOT : (i + 1) * SLOT] = jnp.concatenate(parts, axis=0).astype(BF)
            return start + cnt_ref[0, k]

        lax.fori_loop(0, n_lev, body, jnp.int32(0), unroll=4)

    def ship(c):
        @pl.loop(0, n_lev - 1)
        def _(i):
            peer = peer_of(i)
            pltpu.make_async_remote_copy(
                src_ref=send.at[c, peer],
                dst_ref=recv.at[c, me],
                send_sem=send_sem.at[c],
                recv_sem=recv_sem.at[c],
                device_id={"lev": peer},
                device_id_type=MESH,
            ).start()

        pltpu.make_async_copy(send.at[c, me], recv.at[c, me], recv_sem.at[c]).start()

    adv[tiles] = jnp.zeros(adv.shape[1:], F32)
    for r in range(rows):
        make_side(r)
    for j in range(1, rows):
        make_face(j)
    sweep(value, range(1, 7), first_step)
    sweep(guess, range(2, 6), second_step)
    compact(0)

    pl.semaphore_wait(barrier, n_lev + 1)

    halos = [
        pltpu.make_async_remote_copy(
            src_ref=src,
            dst_ref=dst,
            send_sem=halo_send.at[i],
            recv_sem=halo_recv.at[i],
            device_id={"lat": other},
            device_id_type=MESH,
        )
        for i, (src, dst, other) in enumerate(((up_buf, lo_buf, up), (down_buf, hi_buf, down)))
    ]
    for halo in halos:
        halo.start()
    ship(0)
    compact(1)
    ship(1)

    for halo in halos:
        halo.wait()
    for r in (-1, rows):
        make_side(r)
    for j in (-1, 0, rows, rows + 1):
        make_face(j)
    sweep(value, (-1, 0), first_step)
    sweep(value, (7, 8), first_step)
    sweep(guess, (0, 1), second_step)
    compact(2)
    ship(2)
    sweep(guess, (6, 7), second_step)
    compact(3)
    ship(3)

    def iota(shape, dim):
        return lax.broadcasted_iota(jnp.int32, shape, dim)

    def hot(mask):
        return jnp.where(mask, 1.0, 0.0).astype(BF)

    def field_of(p):
        return lax.rem(p // levels, fields_count)

    def level_of(p):
        return (p // group) * levels + lax.rem(p, levels)

    def dot(a, b, dims=((1,), (0,))):
        return lax.dot_general(a, b, (dims, ((), ())), preferred_element_type=F32)

    for load in loads:
        load.wait()
    p_col = iota((feats, feats), 0)
    order = hot(field_of(p_col) * lev_total + level_of(p_col) == iota((feats, feats), 1))
    expand = hot(level_of(iota((feats, lev_total), 0)) == iota((feats, lev_total), 1))
    spread = dot(dot(expand, rw_in[...]).astype(BF), expand, ((1,), (1,)))
    same = field_of(iota((feats, feats), 0)) == field_of(iota((feats, feats), 1))
    mix[...] = jnp.where(same, spread, 0.0).astype(BF)
    w1t[...] = dot(order, w1_in[...]).T.astype(BF)
    w2t[...] = w2_in[...].astype(F32).T.astype(BF)
    w3t[...] = dot(order, w3_in[...].astype(F32).T.astype(BF)).astype(BF)

    def silu(x):
        return x / (1.0 + jnp.exp(-x))

    for c, pair in enumerate(chunks):
        pltpu.make_async_copy(recv.at[c], recv.at[c], recv_sem.at[c]).wait()
        block = recv[c].reshape(feats, 2 * SLOT)
        remapped = block.astype(F32) + dot(mix[...], block)
        hidden = silu(dot(w1t[...], remapped.astype(BF))).astype(BF)
        hidden = silu(dot(w2t[...], hidden)).astype(BF)
        tendency = dot(w3t[...], hidden).astype(BF).astype(F32)
        for i, r in enumerate(pair):
            hit = jnp.max(jnp.where(grp_ref[...] == lat * rows + r, 1.0, 0.0), keepdims=True)
            part = slice(i * SLOT, (i + 1) * SLOT)
            done[pl.ds(r, feats, stride=rows), :] = remapped[:, part] + hit * tendency[:, part]

    keep = lane < cnt_ref[0, me]

    @pl.loop(0, n_lev)
    def _(src):
        for q in range(group):
            tile = done[pl.ds(pl.multiple_of((src * group + q) * rows, rows), rows), :]
            out_ref[q // levels, src * levels + q % levels] = jnp.where(keep, tile, 0.0).astype(BF)

    for c in range(len(chunks)):
        sent = send.at[c, pl.ds(0, n_lev - 1)]
        pltpu.make_async_copy(sent, sent, send_sem.at[c]).wait()


def shards(n_lat, n_lev, x_size, fields, winds, remap_weight, w_first, w_second, w_third, lon_counts, group_list):
    field_count, levels, rows, lon = fields.shape
    group = field_count * levels
    lev_total = remap_weight.shape[0]
    feats = group * n_lev
    hid = w_first.shape[1]
    halves = group // 8
    hbm = pl.BlockSpec(memory_space=pltpu.HBM)
    vmem = pl.BlockSpec(memory_space=pltpu.VMEM)
    plane = (8, lon)
    halo = (2 * halves + 2,) + plane
    return pl.pallas_call(
        functools.partial(kernel, n_lat, n_lev, x_size, lev_total),
        out_shape=jax.ShapeDtypeStruct((field_count, lev_total, rows, SLOT), BF),
        in_specs=[pl.BlockSpec(memory_space=pltpu.SMEM), vmem, hbm, hbm, hbm, hbm, hbm, hbm],
        out_specs=vmem,
        scratch_shapes=[
            pltpu.VMEM(halo, F32), pltpu.VMEM(halo, F32),
            pltpu.VMEM(halo, F32), pltpu.VMEM(halo, F32),
            pltpu.VMEM((lon // SLOT, group * rows, SLOT), F32),
            pltpu.VMEM((lon // SLOT, 2 * levels * rows, SLOT), F32),
            pltpu.VMEM((rows, halves) + plane, F32),
            pltpu.VMEM((rows,) + plane, F32), pltpu.VMEM((rows,) + plane, F32),
            pltpu.VMEM((rows + 2,) + plane, F32), pltpu.VMEM((rows + 2,) + plane, F32),
            pltpu.VMEM((rows + 3,) + plane, F32), pltpu.VMEM((rows + 3,) + plane, F32),
            pltpu.VMEM((rows + 2, halves) + plane, F32),
            pltpu.VMEM((lon // SLOT + 1, rows, halves, 8, SLOT), F32),
            pltpu.VMEM((4, n_lev, group, 2 * SLOT), BF),
            pltpu.VMEM((4, n_lev, group, 2 * SLOT), BF),
            pltpu.VMEM(remap_weight.shape, BF), pltpu.VMEM(w_first.shape, BF),
            pltpu.VMEM(w_second.shape, BF), pltpu.VMEM(w_third.shape, BF),
            pltpu.VMEM((feats, feats), BF), pltpu.VMEM((hid, feats), BF),
            pltpu.VMEM((hid, hid), BF), pltpu.VMEM((feats, hid), BF),
            pltpu.VMEM((feats * rows, SLOT), F32),
            pltpu.SemaphoreType.DMA((2,)), pltpu.SemaphoreType.DMA((2,)),
            pltpu.SemaphoreType.DMA((4,)), pltpu.SemaphoreType.DMA((4,)),
            pltpu.SemaphoreType.DMA((4,)), pltpu.SemaphoreType.DMA((2, lon // SLOT)),
        ],
        compiler_params=pltpu.CompilerParams(
            collective_id=0, has_side_effects=True, vmem_limit_bytes=48 * 1024 * 1024
        ),
    )(
        lon_counts, group_list, fields.reshape(group * rows, lon), winds.reshape(2 * levels * rows, lon),
        remap_weight, w_first, w_second, w_third,
    )


def solution(mesh):
    n_lat, n_lev = mesh.shape["lat"], mesh.shape["lev"]
    in_specs = (
        P(None, "lev", "lat", None),
        P(None, "lev", "lat", None),
        P(), P(), P(), P(),
        P("lat", None),
        P(),
    )
    return jax.shard_map(
        functools.partial(shards, n_lat, n_lev, 4),
        mesh=mesh,
        in_specs=in_specs,
        out_specs=P(None, None, "lat", "lev"),
        check_vma=False,
    )
```

time: 173 us -> 50 us (0.29)
  the two profiles are of different devices: /device:TPU:27 before, /device:TPU:1 now
where the time goes in v1:
time: 50 us; the launch traced here: 49.6 us
  Pallas kernels  41.9 us (84%)
  local copies, waits for them, and re-layouts  7.66 us (15%)
    pallas_call x1, Pallas kernels, shards(): pl.pallas_call(functools.partial(kernel, n_lat, n_lev, x_size, lev_total)...  41.9 us
    unnamed x16, local copies, waits for them, and re-layouts  7.66 us

profile of v1, /device:TPU:1, one launch (start us, length us, event | category | flops | bytes accessed | tf_op | source)
XLA Modules:
  0.0 49.6 jit_solution(335592644117137170)
XLA Ops:
  0.0 0.0 copy-start.6
  0.0 0.8 %copy.9.grp_ref = s32[16,6]{1,0:T(8,128)S(1)} copy(s32[16,6]{0,1:T(8,128)} %param.15) | data formatting | bytes 768 | tf_op args[7]
  0.8 0.0 copy-done.6
  0.8 0.0 copy-start
  0.8 1.1 %copy-done = f32[4,4,8,1152]{3,2,1,0:T(8,128)S(1)} copy-done((f32[4,4,8,1152]{3,2,1,0:T(8,128)S(1)}, f32[4,4,8,1152]{3,2,1,0:T(8,128)}, u32[]{:S(2)}) %copy-start) | copy-done | bytes 589848
  1.8 0.0 copy-start.1
  1.8 1.0 %copy-done.1 = bf16[512,512]{1,0:T(8,128)(2,1)S(1)} copy-done((bf16[512,512]{1,0:T(8,128)(2,1)S(1)}, bf16[512,512]{1,0:T(8,128)(2,1)}, u32[]{:S(2)}) %copy-start.1) | copy-done | bytes 524312
  2.9 0.0 copy-start.2
  2.9 1.0 %copy-done.2 = bf16[512,512]{1,0:T(8,128)(2,1)S(1)} copy-done((bf16[512,512]{1,0:T(8,128)(2,1)S(1)}, bf16[512,512]{1,0:T(8,128)(2,1)}, u32[]{:S(2)}) %copy-start.2) | copy-done | bytes 524312
  3.9 0.0 copy-start.3
  3.9 1.0 %copy-done.3 = bf16[512,512]{1,0:T(8,128)(2,1)S(1)} copy-done((bf16[512,512]{1,0:T(8,128)(2,1)S(1)}, bf16[512,512]{1,0:T(8,128)(2,1)}, u32[]{:S(2)}) %copy-start.3) | copy-done | bytes 524312
  5.0 0.0 copy-start.4
  5.0 1.0 %copy-done.4 = f32[2,4,8,1152]{3,2,1,0:T(8,128)S(1)} copy-done((f32[2,4,8,1152]{3,2,1,0:T(8,128)S(1)}, f32[2,4,8,1152]{3,2,1,0:T(8,128)}, u32[]{:S(2)}) %copy-start.4) | copy-done | bytes 294936
  5.9 0.0 copy-start.5
  5.9 0.8 %copy-done.5 = bf16[128,128]{1,0:T(8,128)(2,1)S(1)} copy-done((bf16[128,128]{1,0:T(8,128)(2,1)S(1)}, bf16[128,128]{1,0:T(8,128)(2,1)}, u32[]{:S(2)}) %copy-start.5) | copy-done | bytes 32792
  6.7 41.9 %shard_map.82 = bf16[4,128,8,128]{3,2,1,0:T(8,128)(2,1)S(1)} custom-call(s32[1,32]{1,0:T(1,128)S(1)} %copy-done.6, s32[16,6]{1,0:T(8,128)S(1)} %copy.9.grp_ref, f32[128,1152]{1,0:T(8,128)S(1)} %bitcast.2, f32[64,1152]{1,0:T(8,128)S(1)} %bitcast.3, bf16[128,128]{1,0:T(8,128)(2,1)S(1)} %copy-done.5, bf16[512,512]{1,0:T(8,128)(2,1)S(1)} %copy-done.1, ...), custom_call_target="tpu_custom_call" | custom-call | tf_op jit(solution)/shard_map/pallas_call | solution.py:301
  48.6 1.0 %copy.11 = bf16[4,128,8,128]{3,2,1,0:T(8,128)(2,1)} copy(bf16[4,128,8,128]{3,2,1,0:T(8,128)(2,1)S(1)} %shard_map.82) | data formatting | bytes 2097152
Async XLA Ops:
  0.0 0.8 %copy-start.6 = (s32[1,32]{1,0:T(1,128)S(1)}, s32[1,32]{1,0:T(1,128)}, u32[]{:S(2)}) copy-start(s32[1,32]{1,0:T(1,128)} %cnt_ref.1) | copy-start | bytes 388
  0.8 1.1 %copy-start = (f32[4,4,8,1152]{3,2,1,0:T(8,128)S(1)}, f32[4,4,8,1152]{3,2,1,0:T(8,128)}, u32[]{:S(2)}) copy-start(f32[4,4,8,1152]{3,2,1,0:T(8,128)} %param.8) | copy-start | bytes 1769476
  1.8 1.0 %copy-start.1 = (bf16[512,512]{1,0:T(8,128)(2,1)S(1)}, bf16[512,512]{1,0:T(8,128)(2,1)}, u32[]{:S(2)}) copy-start(bf16[512,512]{1,0:T(8,128)(2,1)} %w1_hbm.1) | copy-start | bytes 1572868
  2.9 1.0 %copy-start.2 = (bf16[512,512]{1,0:T(8,128)(2,1)S(1)}, bf16[512,512]{1,0:T(8,128)(2,1)}, u32[]{:S(2)}) copy-start(bf16[512,512]{1,0:T(8,128)(2,1)} %w2_hbm.1) | copy-start | bytes 1572868
  3.9 1.0 %copy-start.3 = (bf16[512,512]{1,0:T(8,128)(2,1)S(1)}, bf16[512,512]{1,0:T(8,128)(2,1)}, u32[]{:S(2)}) copy-start(bf16[512,512]{1,0:T(8,128)(2,1)} %w3_hbm.1) | copy-start | bytes 1572868
  5.0 1.0 %copy-start.4 = (f32[2,4,8,1152]{3,2,1,0:T(8,128)S(1)}, f32[2,4,8,1152]{3,2,1,0:T(8,128)}, u32[]{:S(2)}) copy-start(f32[2,4,8,1152]{3,2,1,0:T(8,128)} %param.9) | copy-start | bytes 884740
  5.9 0.8 %copy-start.5 = (bf16[128,128]{1,0:T(8,128)(2,1)S(1)}, bf16[128,128]{1,0:T(8,128)(2,1)}, u32[]{:S(2)}) copy-start(bf16[128,128]{1,0:T(8,128)(2,1)} %rw_hbm.1) | copy-start | bytes 98308

commit v2 on v1

--- a/solution.py
+++ b/solution.py
@@ -9,6 +9,7 @@
 
 DIFFUSION = 0.15
 SLOT = 128
+LIMIT = 48000000
 MESH = pl.DeviceIdType.MESH
 BF = jnp.bfloat16
 F32 = jnp.float32
@@ -16,13 +17,13 @@
 
 def kernel(
     n_lat, n_lev, x_size, lev_total,
-    cnt_ref, grp_ref, fields_hbm, winds_hbm, rw_hbm, w1_hbm, w2_hbm, w3_hbm,
+    cnt_hbm, grp_hbm, fields_hbm, winds_hbm, rw_hbm, w1_hbm, w2_hbm, w3_hbm,
     out_ref,
     up_buf, down_buf, lo_buf, hi_buf,
     tracer, wind_in, sown, ew, nw, ah, bh, ag, bg, pred, adv,
     send, recv,
     rw_in, w1_in, w2_in, w3_in, mix, w1t, w2t, w3t, done,
-    halo_send, halo_recv, send_sem, recv_sem, load_sem, in_sem,
+    halo_send, halo_recv, send_sem, recv_sem, load_sem, in_sem, cnt_ref, grp_ref,
 ):
     rows, fields_count = 8, 4
     group = send.shape[2]
@@ -64,7 +65,7 @@
     loads = [
         pltpu.make_async_copy(src, dst, load_sem.at[i])
         for i, (src, dst) in enumerate(
-            ((rw_hbm, rw_in), (w1_hbm, w1_in), (w2_hbm, w2_in), (w3_hbm, w3_in))
+            ((cnt_hbm, cnt_ref), (grp_hbm, grp_ref), (rw_hbm, rw_in), (w1_hbm, w1_in), (w2_hbm, w2_in), (w3_hbm, w3_in))
         )
     ]
     for load in loads:
@@ -196,6 +197,7 @@
         make_face(j)
     sweep(value, range(1, 7), first_step)
     sweep(guess, range(2, 6), second_step)
+    loads[0].wait()
     compact(0)
 
     pl.semaphore_wait(barrier, n_lev + 1)
@@ -247,7 +249,7 @@
     def dot(a, b, dims=((1,), (0,))):
         return lax.dot_general(a, b, (dims, ((), ())), preferred_element_type=F32)
 
-    for load in loads:
+    for load in loads[1:]:
         load.wait()
     p_col = iota((feats, feats), 0)
     order = hot(field_of(p_col) * lev_total + level_of(p_col) == iota((feats, feats), 1))
@@ -293,6 +295,7 @@
     lev_total = remap_weight.shape[0]
     feats = group * n_lev
     hid = w_first.shape[1]
+    group_list = group_list.T
     halves = group // 8
     hbm = pl.BlockSpec(memory_space=pltpu.HBM)
     vmem = pl.BlockSpec(memory_space=pltpu.VMEM)
@@ -301,7 +304,7 @@
     return pl.pallas_call(
         functools.partial(kernel, n_lat, n_lev, x_size, lev_total),
         out_shape=jax.ShapeDtypeStruct((field_count, lev_total, rows, SLOT), BF),
-        in_specs=[pl.BlockSpec(memory_space=pltpu.SMEM), vmem, hbm, hbm, hbm, hbm, hbm, hbm],
+        in_specs=[hbm, hbm, hbm, hbm, hbm, hbm, hbm, hbm],
         out_specs=vmem,
         scratch_shapes=[
             pltpu.VMEM(halo, F32), pltpu.VMEM(halo, F32),
@@ -323,15 +326,16 @@
             pltpu.VMEM((feats * rows, SLOT), F32),
             pltpu.SemaphoreType.DMA((2,)), pltpu.SemaphoreType.DMA((2,)),
             pltpu.SemaphoreType.DMA((4,)), pltpu.SemaphoreType.DMA((4,)),
-            pltpu.SemaphoreType.DMA((4,)), pltpu.SemaphoreType.DMA((2, lon // SLOT)),
+            pltpu.SemaphoreType.DMA((6,)), pltpu.SemaphoreType.DMA((2, lon // SLOT)),
+            pltpu.SMEM(lon_counts.shape, jnp.int32), pltpu.VMEM(group_list.shape, jnp.int32),
         ],
         compiler_params=pltpu.CompilerParams(
-            collective_id=0, has_side_effects=True, vmem_limit_bytes=48 * 1024 * 1024
+            collective_id=0, has_side_effects=True, vmem_limit_bytes=LIMIT
         ),
-    )(
+    )(*(pltpu.with_memory_space_constraint(x, pltpu.HBM) for x in (
         lon_counts, group_list, fields.reshape(group * rows, lon), winds.reshape(2 * levels * rows, lon),
         remap_weight, w_first, w_second, w_third,
-    )
+    )))
 
 
 def solution(mesh):

time: 50 us -> 43.5 us (0.87)
  local copies, waits for them, and re-layouts: 7.66 us -> 0.97 us
    unnamed x16 -> x1, local copies, waits for them, and re-layouts: 7.66 us -> 0.97 us
where the time goes in v2:
time: 43.5 us; the launch traced here: 43.3 us
  Pallas kernels  42.3 us (97%)
  local copies, waits for them, and re-layouts  0.97 us (2%)
    pallas_call x1, Pallas kernels, shards(): pl.pallas_call(functools.partial(kernel, n_lat, n_lev, x_size, lev_total)...  42.3 us
    unnamed x1, local copies, waits for them, and re-layouts  0.97 us

profile of v2, /device:TPU:1, one launch (start us, length us, event | category | flops | bytes accessed | tf_op | source)
XLA Modules:
  0.0 43.3 jit_solution(1800743918504611526)
XLA Ops:
  0.0 42.3 %shard_map.82 = bf16[4,128,8,128]{3,2,1,0:T(8,128)(2,1)S(1)} custom-call(s32[1,32]{1,0:T(1,128)} %cnt_hbm.1, s32[6,16]{1,0:T(8,128)} %bitcast.5, f32[128,1152]{1,0:T(8,128)} %bitcast.3, f32[64,1152]{1,0:T(8,128)} %bitcast.4, bf16[128,128]{1,0:T(8,128)(2,1)} %rw_hbm.1, bf16[512,512]{1,0:T(8,128)(2,1)} %w1_hbm.1, bf16[512,512]{1,0:T(8,128)(2,1)} %w2_hbm.1, ...), custom_call_target="tpu_custom_call" | custom-call | tf_op jit(solution)/shard_map/pallas_call | solution.py:304
  42.4 1.0 %copy.10 = bf16[4,128,8,128]{3,2,1,0:T(8,128)(2,1)} copy(bf16[4,128,8,128]{3,2,1,0:T(8,128)(2,1)S(1)} %shard_map.82) | data formatting | bytes 2097152

commit v3 on v2

--- a/solution.py
+++ b/solution.py
@@ -9,6 +9,7 @@
 
 DIFFUSION = 0.15
 SLOT = 128
+X_SIZE = 4
 LIMIT = 48000000
 MESH = pl.DeviceIdType.MESH
 BF = jnp.bfloat16
@@ -20,10 +21,10 @@
     cnt_hbm, grp_hbm, fields_hbm, winds_hbm, rw_hbm, w1_hbm, w2_hbm, w3_hbm,
     out_ref,
     up_buf, down_buf, lo_buf, hi_buf,
-    tracer, wind_in, sown, ew, nw, ah, bh, ag, bg, pred, adv,
-    send, recv,
+    tracer, wind_in, sown, ew, nw, ah, bh, ag, bg, pred,
+    raw_out, starts, send, recv,
     rw_in, w1_in, w2_in, w3_in, mix, w1t, w2t, w3t, done,
-    halo_send, halo_recv, send_sem, recv_sem, load_sem, in_sem, cnt_ref, grp_ref,
+    halo_send, halo_recv, send_sem, recv_sem, raw_send, raw_recv, load_sem, in_sem, cnt_ref, grp_ref, *raw_in,
 ):
     rows, fields_count = 8, 4
     group = send.shape[2]
@@ -38,19 +39,30 @@
     up, down = lax.rem(lat + 1, n_lat), lax.rem(lat + n_lat - 1, n_lat)
     z_size = n_lev // x_size
     my_z, my_x = me // x_size, lax.rem(me, x_size)
-
-    def peer_of(i):
-        step, dx = i // x_size, lax.rem(i, x_size) + 1
-        dz = z_size // 2 + (1 - 2 * lax.rem(step, 2)) * ((step + 1) // 2)
-        return lax.rem(my_z + dz, z_size) * x_size + lax.rem(my_x + dx, x_size)
+    reach = z_size // 2 - 1
+    below, above = lax.rem(my_z + z_size - 1, z_size), lax.rem(my_z + 1, z_size)
+
+    def place(z, x):
+        return lax.rem(z, z_size) * x_size + lax.rem(x, x_size)
 
     barrier = pltpu.get_barrier_semaphore()
+
+    def greet(where):
+        pl.semaphore_signal(barrier, inc=1, device_id=where, device_id_type=MESH)
+
     for other in (up, down):
-        pl.semaphore_signal(barrier, inc=1, device_id={"lat": other}, device_id_type=MESH)
-
-    @pl.loop(0, n_lev - 1)
+        greet({"lat": other})
+
+    @pl.loop(0, reach * x_size)
     def _(i):
-        pl.semaphore_signal(barrier, inc=1, device_id={"lev": peer_of(i)}, device_id_type=MESH)
+        greet({"lev": place(my_z + 1 + i // x_size, i)})
+        greet({"lev": place(my_z + z_size - 1 - i // x_size, i)})
+
+    @pl.loop(1, x_size)
+    def _(i):
+        greet({"lev": place(my_z, my_x + i)})
+
+    greeted = 2 + 2 * reach * x_size + x_size - 1
 
     tiles = lon // SLOT
     columns = [slice(t * SLOT, (t + 1) * SLOT) for t in range(tiles)]
@@ -148,49 +160,107 @@
     def first_step(r, h, here, change):
         pred[r + 1, h] = here + change
 
+    slot_of = {r: (c, i) for c, pair in enumerate(chunks) for i, r in enumerate(pair)}
+
     def second_step(r, h, here, change):
-        result = 0.5 * (value(r, h) + here + change)
+        c, i = slot_of[r]
+        result = (0.5 * (value(r, h) + here + change)).astype(BF)
         for t, part in enumerate(columns):
-            adv[t, r, h] = result[:, part]
+            raw_out[c, t, i, 8 * h : 8 * h + 8, :] = result[:, part]
 
     def guess(r, h):
         return pred[r + 1, h]
 
-    lane = lax.broadcasted_iota(jnp.int32, (8, SLOT), 1)
-
-    def compact(c):
-        def body(k, start):
+    lane = lax.broadcasted_iota(jnp.int32, (group, SLOT), 1)
+    last_bit = (tiles - 1).bit_length() - 1
+    to_right = [reach + 1 if c % 2 == 0 else reach for c in range(len(chunks))]
+
+    def first_slot(c, way):
+        return (0, x_size, x_size * (1 + to_right[c]))[way]
+
+    def planes(c, way):
+        return (1, to_right[c], 2 * reach + 1 - to_right[c])[way]
+
+    def plane_of(way, j):
+        return my_z + z_size - j if way == 2 else my_z + j
+
+    def source_of(way):
+        return (me, below * x_size + my_x, above * x_size + my_x)[way]
+
+    def pack(c, way):
+        base = first_slot(c, way)
+
+        def body(i, carry):
+            start = starts[0, place(plane_of(way, i // x_size), i)]
             tile = start >> 7
+            after = (tile + 1) - (tile >> last_bit)
             shift = start & (SLOT - 1)
             back = (SLOT - shift) & (SLOT - 1)
             take = lane < SLOT - shift
-            for i, r in enumerate(chunks[c]):
-                parts = []
-                for h in range(halves):
-                    a = pltpu.roll(adv[tile, r, h], back, axis=1)
-                    b = pltpu.roll(adv[tile + 1, r, h], back, axis=1)
-                    parts.append(jnp.where(take, a, b))
-                send[c, k, :, i * SLOT : (i + 1) * SLOT] = jnp.concatenate(parts, axis=0).astype(BF)
-            return start + cnt_ref[0, k]
-
-        lax.fori_loop(0, n_lev, body, jnp.int32(0), unroll=4)
-
-    def ship(c):
-        @pl.loop(0, n_lev - 1)
+            for k in range(2):
+                if way == 0:
+                    a, b = raw_out[c, tile, k], raw_out[c, after, k]
+                else:
+                    arrived = raw_in[2 * c + way - 1]
+                    a, b = arrived[tile, k], arrived[after, k]
+                a, b = pltpu.roll(a, back, axis=1), pltpu.roll(b, back, axis=1)
+                send[c, base + i, :, k * SLOT : (k + 1) * SLOT] = jnp.where(take, a, b)
+            return carry
+
+        count = planes(c, way) * x_size
+        lax.fori_loop(0, count, body, 0, unroll=4 if count % 4 == 0 else 1)
+
+    def slot_copy(c, way, j, x):
+        source = source_of(way)
+        x = lax.rem(x, x_size)
+        return pltpu.make_async_remote_copy(
+            src_ref=send.at[c, first_slot(c, way) + j * x_size + x],
+            dst_ref=recv.at[c, source],
+            send_sem=send_sem.at[c],
+            recv_sem=recv_sem.at[c],
+            device_id={"lev": place(plane_of(way, j), x)},
+            device_id_type=MESH,
+        )
+
+    def ship(c, way):
+        far = planes(c, way) - 1
+        if far > 0:
+
+            @pl.loop(0, far * x_size)
+            def _(i):
+                slot_copy(c, way, far - i // x_size, i).start()
+
+        @pl.loop(1, x_size)
         def _(i):
-            peer = peer_of(i)
-            pltpu.make_async_remote_copy(
-                src_ref=send.at[c, peer],
-                dst_ref=recv.at[c, me],
-                send_sem=send_sem.at[c],
-                recv_sem=recv_sem.at[c],
-                device_id={"lev": peer},
-                device_id_type=MESH,
-            ).start()
-
-        pltpu.make_async_copy(send.at[c, me], recv.at[c, me], recv_sem.at[c]).start()
-
-    adv[tiles] = jnp.zeros(adv.shape[1:], F32)
+            slot_copy(c, way, 0, my_x + i).start()
+
+        mine = send.at[c, first_slot(c, way) + my_x]
+        pltpu.make_async_copy(mine, recv.at[c, source_of(way)], recv_sem.at[c]).start()
+
+    def raw_copy(c, w):
+        return pltpu.make_async_remote_copy(
+            src_ref=raw_out.at[c],
+            dst_ref=raw_in[2 * c + w],
+            send_sem=raw_send.at[w, c],
+            recv_sem=raw_recv.at[w, c],
+            device_id={"lev": (above, below)[w] * x_size + my_x},
+            device_id_type=MESH,
+        )
+
+    def send_raw(c):
+        for w in (0, 1):
+            raw_copy(c, w).start()
+
+    def relay(c):
+        for w in (0, 1):
+            raw_copy(c, w).wait_recv()
+            pack(c, w + 1)
+            ship(c, w + 1)
+
+    def own(c):
+        pack(c, 0)
+        ship(c, 0)
+
     for r in range(rows):
         make_side(r)
     for j in range(1, rows):
@@ -198,9 +268,14 @@
     sweep(value, range(1, 7), first_step)
     sweep(guess, range(2, 6), second_step)
     loads[0].wait()
-    compact(0)
-
-    pl.semaphore_wait(barrier, n_lev + 1)
+
+    def prefix(k, start):
+        starts[0, k] = start
+        return start + cnt_ref[0, k]
+
+    lax.fori_loop(0, n_lev, prefix, jnp.int32(0))
+
+    pl.semaphore_wait(barrier, greeted)
 
     halos = [
         pltpu.make_async_remote_copy(
@@ -215,9 +290,11 @@
     ]
     for halo in halos:
         halo.start()
-    ship(0)
-    compact(1)
-    ship(1)
+    send_raw(0)
+    send_raw(1)
+    own(0)
+    own(1)
+    relay(0)
 
     for halo in halos:
         halo.wait()
@@ -226,13 +303,14 @@
     for j in (-1, 0, rows, rows + 1):
         make_face(j)
     sweep(value, (-1, 0), first_step)
+    sweep(guess, (0, 1), second_step)
+    send_raw(2)
     sweep(value, (7, 8), first_step)
-    sweep(guess, (0, 1), second_step)
-    compact(2)
-    ship(2)
     sweep(guess, (6, 7), second_step)
-    compact(3)
-    ship(3)
+    send_raw(3)
+    own(2)
+    own(3)
+    relay(1)
 
     def iota(shape, dim):
         return lax.broadcasted_iota(jnp.int32, shape, dim)
@@ -261,6 +339,9 @@
     w2t[...] = w2_in[...].astype(F32).T.astype(BF)
     w3t[...] = dot(order, w3_in[...].astype(F32).T.astype(BF)).astype(BF)
 
+    relay(2)
+    relay(3)
+
     def silu(x):
         return x / (1.0 + jnp.exp(-x))
 
@@ -276,7 +357,7 @@
             part = slice(i * SLOT, (i + 1) * SLOT)
             done[pl.ds(r, feats, stride=rows), :] = remapped[:, part] + hit * tendency[:, part]
 
-    keep = lane < cnt_ref[0, me]
+    keep = lane[:8] < cnt_ref[0, me]
 
     @pl.loop(0, n_lev)
     def _(src):
@@ -285,8 +366,10 @@
             out_ref[q // levels, src * levels + q % levels] = jnp.where(keep, tile, 0.0).astype(BF)
 
     for c in range(len(chunks)):
-        sent = send.at[c, pl.ds(0, n_lev - 1)]
+        sent = send.at[c, pl.ds(0, n_lev - 3)]
         pltpu.make_async_copy(sent, sent, send_sem.at[c]).wait()
+        for w in (0, 1):
+            raw_copy(c, w).wait_send()
 
 
 def shards(n_lat, n_lev, x_size, fields, winds, remap_weight, w_first, w_second, w_third, lon_counts, group_list):
@@ -316,7 +399,8 @@
             pltpu.VMEM((rows + 2,) + plane, F32), pltpu.VMEM((rows + 2,) + plane, F32),
             pltpu.VMEM((rows + 3,) + plane, F32), pltpu.VMEM((rows + 3,) + plane, F32),
             pltpu.VMEM((rows + 2, halves) + plane, F32),
-            pltpu.VMEM((lon // SLOT + 1, rows, halves, 8, SLOT), F32),
+            pltpu.VMEM((4, lon // SLOT, 2, group, SLOT), BF),
+            pltpu.SMEM((1, n_lev), jnp.int32),
             pltpu.VMEM((4, n_lev, group, 2 * SLOT), BF),
             pltpu.VMEM((4, n_lev, group, 2 * SLOT), BF),
             pltpu.VMEM(remap_weight.shape, BF), pltpu.VMEM(w_first.shape, BF),
@@ -326,8 +410,10 @@
             pltpu.VMEM((feats * rows, SLOT), F32),
             pltpu.SemaphoreType.DMA((2,)), pltpu.SemaphoreType.DMA((2,)),
             pltpu.SemaphoreType.DMA((4,)), pltpu.SemaphoreType.DMA((4,)),
+            pltpu.SemaphoreType.DMA((2, 4)), pltpu.SemaphoreType.DMA((2, 4)),
             pltpu.SemaphoreType.DMA((6,)), pltpu.SemaphoreType.DMA((2, lon // SLOT)),
             pltpu.SMEM(lon_counts.shape, jnp.int32), pltpu.VMEM(group_list.shape, jnp.int32),
+            *[pltpu.VMEM((lon // SLOT, 2, group, SLOT), BF)] * 8,
         ],
         compiler_params=pltpu.CompilerParams(
             collective_id=0, has_side_effects=True, vmem_limit_bytes=LIMIT
@@ -348,7 +434,7 @@
         P(),
     )
     return jax.shard_map(
-        functools.partial(shards, n_lat, n_lev, 4),
+        functools.partial(shards, n_lat, n_lev, X_SIZE),
         mesh=mesh,
         in_specs=in_specs,
         out_specs=P(None, None, "lat", "lev"),

time: 43.5 us -> 39 us (0.90); the launches traced: 43.3 us -> 38.3 us
  Pallas kernels: 42.3 us -> 37.3 us
    pallas_call x1, Pallas kernels: 42.3 us -> 37.3 us  [shards(): pl.pallas_call(functools.partial(kernel, n_lat, n_lev, x_size, lev_total)...]
where the time goes in v3:
time: 39 us; the launch traced here: 38.3 us
  Pallas kernels  37.3 us (96%)
  local copies, waits for them, and re-layouts  0.97 us (2%)
    pallas_call x1, Pallas kernels, shards(): pl.pallas_call(functools.partial(kernel, n_lat, n_lev, x_size, lev_total)...  37.3 us
    unnamed x1, local copies, waits for them, and re-layouts  0.97 us

profile of v3, /device:TPU:1, one launch (start us, length us, event | category | flops | bytes accessed | tf_op | source)
XLA Modules:
  0.0 38.3 jit_solution(16426314843797486094)
XLA Ops:
  0.0 37.3 %shard_map.82 = bf16[4,128,8,128]{3,2,1,0:T(8,128)(2,1)S(1)} custom-call(s32[1,32]{1,0:T(1,128)} %cnt_hbm.1, s32[6,16]{1,0:T(8,128)} %bitcast.5, f32[128,1152]{1,0:T(8,128)} %bitcast.3, f32[64,1152]{1,0:T(8,128)} %bitcast.4, bf16[128,128]{1,0:T(8,128)(2,1)} %rw_hbm.1, bf16[512,512]{1,0:T(8,128)(2,1)} %w1_hbm.1, bf16[512,512]{1,0:T(8,128)(2,1)} %w2_hbm.1, ...), custom_call_target="tpu_custom_call" | custom-call | tf_op jit(solution)/shard_map/pallas_call | solution.py:387
  37.3 1.0 %copy.10 = bf16[4,128,8,128]{3,2,1,0:T(8,128)(2,1)} copy(bf16[4,128,8,128]{3,2,1,0:T(8,128)(2,1)S(1)} %shard_map.82) | data formatting | bytes 2097152

commit v4 on v3

--- a/solution.py
+++ b/solution.py
@@ -24,7 +24,7 @@
     tracer, wind_in, sown, ew, nw, ah, bh, ag, bg, pred,
     raw_out, starts, send, recv,
     rw_in, w1_in, w2_in, w3_in, mix, w1t, w2t, w3t, done,
-    halo_send, halo_recv, send_sem, recv_sem, raw_send, raw_recv, load_sem, in_sem, cnt_ref, grp_ref, *raw_in,
+    halo_send, halo_recv, send_sem, recv_sem, raw_send, raw_recv, fwd_send, fwd_recv, load_sem, in_sem, cnt_ref, grp_ref, *raw_bufs,
 ):
     rows, fields_count = 8, 4
     group = send.shape[2]
@@ -44,25 +44,6 @@
 
     def place(z, x):
         return lax.rem(z, z_size) * x_size + lax.rem(x, x_size)
-
-    barrier = pltpu.get_barrier_semaphore()
-
-    def greet(where):
-        pl.semaphore_signal(barrier, inc=1, device_id=where, device_id_type=MESH)
-
-    for other in (up, down):
-        greet({"lat": other})
-
-    @pl.loop(0, reach * x_size)
-    def _(i):
-        greet({"lev": place(my_z + 1 + i // x_size, i)})
-        greet({"lev": place(my_z + z_size - 1 - i // x_size, i)})
-
-    @pl.loop(1, x_size)
-    def _(i):
-        greet({"lev": place(my_z, my_x + i)})
-
-    greeted = 2 + 2 * reach * x_size + x_size - 1
 
     tiles = lon // SLOT
     columns = [slice(t * SLOT, (t + 1) * SLOT) for t in range(tiles)]
@@ -73,6 +54,27 @@
         inputs.append(pltpu.make_async_copy(winds_hbm.at[:, cut], wind_in.at[t], in_sem.at[1, t]))
     for copy in inputs:
         copy.start()
+
+    barrier = pltpu.get_barrier_semaphore()
+
+    def greet(where):
+        pl.semaphore_signal(barrier, inc=1, device_id=where, device_id_type=MESH)
+
+    for other in (up, down):
+        greet({"lat": other})
+
+    near = max(1, reach - 1)
+
+    @pl.loop(0, near * x_size)
+    def _(i):
+        greet({"lev": place(my_z + 1 + i // x_size, i)})
+        greet({"lev": place(my_z + z_size - 1 - i // x_size, i)})
+
+    @pl.loop(1, x_size)
+    def _(i):
+        greet({"lev": place(my_z, my_x + i)})
+
+    greeted = 2 + 2 * near * x_size + x_size - 1
 
     loads = [
         pltpu.make_async_copy(src, dst, load_sem.at[i])
@@ -173,69 +175,63 @@
 
     lane = lax.broadcasted_iota(jnp.int32, (group, SLOT), 1)
     last_bit = (tiles - 1).bit_length() - 1
-    to_right = [reach + 1 if c % 2 == 0 else reach for c in range(len(chunks))]
-
-    def first_slot(c, way):
-        return (0, x_size, x_size * (1 + to_right[c]))[way]
-
-    def planes(c, way):
-        return (1, to_right[c], 2 * reach + 1 - to_right[c])[way]
-
-    def plane_of(way, j):
-        return my_z + z_size - j if way == 2 else my_z + j
-
-    def source_of(way):
-        return (me, below * x_size + my_x, above * x_size + my_x)[way]
-
-    def pack(c, way):
-        base = first_slot(c, way)
+    raw_in, raw_far = raw_bufs[:8], raw_bufs[8:]
+
+    def part_of(c, k):
+        side = c % 2
+        ups = (1 - 2 * side) % z_size
+        nears = [below * x_size + my_x, above * x_size + my_x]
+        if k == 0:
+            return 0, 1, 1, me, raw_out.at[c]
+        if k == 1:
+            return x_size, 1, 1, nears[side], raw_in[2 * c + side]
+        if k == 2:
+            return 2 * x_size, reach, ups, place(my_z + (z_size - 2, 2)[side], 0) + my_x, raw_far[c]
+        return (2 + reach) * x_size, reach, z_size - ups, nears[1 - side], raw_in[2 * c + 1 - side]
+
+    def pack(c, k):
+        base, count, step, _, rows_in = part_of(c, k)
 
         def body(i, carry):
-            start = starts[0, place(plane_of(way, i // x_size), i)]
+            start = starts[0, place(my_z + (i // x_size) * step, i)]
             tile = start >> 7
             after = (tile + 1) - (tile >> last_bit)
             shift = start & (SLOT - 1)
             back = (SLOT - shift) & (SLOT - 1)
             take = lane < SLOT - shift
-            for k in range(2):
-                if way == 0:
-                    a, b = raw_out[c, tile, k], raw_out[c, after, k]
-                else:
-                    arrived = raw_in[2 * c + way - 1]
-                    a, b = arrived[tile, k], arrived[after, k]
-                a, b = pltpu.roll(a, back, axis=1), pltpu.roll(b, back, axis=1)
-                send[c, base + i, :, k * SLOT : (k + 1) * SLOT] = jnp.where(take, a, b)
+            for q in range(2):
+                a = pltpu.roll(rows_in[tile, q], back, axis=1)
+                b = pltpu.roll(rows_in[after, q], back, axis=1)
+                send[c, base + i, :, q * SLOT : (q + 1) * SLOT] = jnp.where(take, a, b)
             return carry
 
-        count = planes(c, way) * x_size
-        lax.fori_loop(0, count, body, 0, unroll=4 if count % 4 == 0 else 1)
-
-    def slot_copy(c, way, j, x):
-        source = source_of(way)
+        lax.fori_loop(0, count * x_size, body, 0, unroll=4 if x_size == 4 else 1)
+
+    def slot_copy(c, k, j, x):
+        base, _, step, source, _ = part_of(c, k)
         x = lax.rem(x, x_size)
         return pltpu.make_async_remote_copy(
-            src_ref=send.at[c, first_slot(c, way) + j * x_size + x],
+            src_ref=send.at[c, base + j * x_size + x],
             dst_ref=recv.at[c, source],
             send_sem=send_sem.at[c],
             recv_sem=recv_sem.at[c],
-            device_id={"lev": place(plane_of(way, j), x)},
+            device_id={"lev": place(my_z + j * step, x)},
             device_id_type=MESH,
         )
 
-    def ship(c, way):
-        far = planes(c, way) - 1
-        if far > 0:
-
-            @pl.loop(0, far * x_size)
+    def ship(c, k):
+        base, count, _, source, _ = part_of(c, k)
+        if count > 1:
+
+            @pl.loop(0, (count - 1) * x_size)
             def _(i):
-                slot_copy(c, way, far - i // x_size, i).start()
+                slot_copy(c, k, count - 1 - i // x_size, i).start()
 
         @pl.loop(1, x_size)
         def _(i):
-            slot_copy(c, way, 0, my_x + i).start()
-
-        mine = send.at[c, first_slot(c, way) + my_x]
-        pltpu.make_async_copy(mine, recv.at[c, source_of(way)], recv_sem.at[c]).start()
+            slot_copy(c, k, 0, my_x + i).start()
+
+        pltpu.make_async_copy(send.at[c, base + my_x], recv.at[c, source], recv_sem.at[c]).start()
 
     def raw_copy(c, w):
         return pltpu.make_async_remote_copy(
@@ -247,33 +243,46 @@
             device_id_type=MESH,
         )
 
+    def forward_copy(c):
+        side = c % 2
+        return pltpu.make_async_remote_copy(
+            src_ref=raw_in[2 * c + side],
+            dst_ref=raw_far[c],
+            send_sem=fwd_send.at[c],
+            recv_sem=fwd_recv.at[c],
+            device_id={"lev": (above, below)[side] * x_size + my_x},
+            device_id_type=MESH,
+        )
+
     def send_raw(c):
         for w in (0, 1):
             raw_copy(c, w).start()
 
     def relay(c):
-        for w in (0, 1):
-            raw_copy(c, w).wait_recv()
-            pack(c, w + 1)
-            ship(c, w + 1)
+        side = c % 2
+        raw_copy(c, side).wait_recv()
+        forward_copy(c).start()
+        pack(c, 1)
+        ship(c, 1)
+        raw_copy(c, 1 - side).wait_recv()
+        pack(c, 3)
+        ship(c, 3)
+
+    def relay_far(c):
+        forward_copy(c).wait_recv()
+        pack(c, 2)
+        ship(c, 2)
 
     def own(c):
         pack(c, 0)
         ship(c, 0)
 
-    for r in range(rows):
+    for r in range(1, 5):
         make_side(r)
-    for j in range(1, rows):
+    for j in range(1, 6):
         make_face(j)
-    sweep(value, range(1, 7), first_step)
-    sweep(guess, range(2, 6), second_step)
-    loads[0].wait()
-
-    def prefix(k, start):
-        starts[0, k] = start
-        return start + cnt_ref[0, k]
-
-    lax.fori_loop(0, n_lev, prefix, jnp.int32(0))
+    sweep(value, range(1, 5), first_step)
+    sweep(guess, (2, 3), second_step)
 
     pl.semaphore_wait(barrier, greeted)
 
@@ -291,7 +300,22 @@
     for halo in halos:
         halo.start()
     send_raw(0)
+    for r in (5, 6):
+        make_side(r)
+    for j in (6, 7):
+        make_face(j)
+    sweep(value, (5, 6), first_step)
+    sweep(guess, (4, 5), second_step)
     send_raw(1)
+    for r in (0, 7):
+        make_side(r)
+    loads[0].wait()
+
+    def prefix(k, start):
+        starts[0, k] = start
+        return start + cnt_ref[0, k]
+
+    lax.fori_loop(0, n_lev, prefix, jnp.int32(0))
     own(0)
     own(1)
     relay(0)
@@ -311,6 +335,8 @@
     own(2)
     own(3)
     relay(1)
+    relay_far(0)
+    relay_far(1)
 
     def iota(shape, dim):
         return lax.broadcasted_iota(jnp.int32, shape, dim)
@@ -341,6 +367,8 @@
 
     relay(2)
     relay(3)
+    relay_far(2)
+    relay_far(3)
 
     def silu(x):
         return x / (1.0 + jnp.exp(-x))
@@ -366,10 +394,11 @@
             out_ref[q // levels, src * levels + q % levels] = jnp.where(keep, tile, 0.0).astype(BF)
 
     for c in range(len(chunks)):
-        sent = send.at[c, pl.ds(0, n_lev - 3)]
+        sent = send.at[c, pl.ds(0, n_lev - 4)]
         pltpu.make_async_copy(sent, sent, send_sem.at[c]).wait()
         for w in (0, 1):
             raw_copy(c, w).wait_send()
+        forward_copy(c).wait_send()
 
 
 def shards(n_lat, n_lev, x_size, fields, winds, remap_weight, w_first, w_second, w_third, lon_counts, group_list):
@@ -411,9 +440,10 @@
             pltpu.SemaphoreType.DMA((2,)), pltpu.SemaphoreType.DMA((2,)),
             pltpu.SemaphoreType.DMA((4,)), pltpu.SemaphoreType.DMA((4,)),
             pltpu.SemaphoreType.DMA((2, 4)), pltpu.SemaphoreType.DMA((2, 4)),
+            pltpu.SemaphoreType.DMA((4,)), pltpu.SemaphoreType.DMA((4,)),
             pltpu.SemaphoreType.DMA((6,)), pltpu.SemaphoreType.DMA((2, lon // SLOT)),
             pltpu.SMEM(lon_counts.shape, jnp.int32), pltpu.VMEM(group_list.shape, jnp.int32),
-            *[pltpu.VMEM((lon // SLOT, 2, group, SLOT), BF)] * 8,
+            *[pltpu.VMEM((lon // SLOT, 2, group, SLOT), BF)] * 12,
         ],
         compiler_params=pltpu.CompilerParams(
             collective_id=0, has_side_effects=True, vmem_limit_bytes=LIMIT

time: 39 us -> 41.6 us (1.067)
  Pallas kernels: 37.3 us -> 40.3 us
    pallas_call x1, Pallas kernels: 37.3 us -> 40.3 us  [shards(): pl.pallas_call(functools.partial(kernel, n_lat, n_lev, x_size, lev_total)...]
where the time goes in v4:
time: 41.6 us; the launch traced here: 41.3 us
  Pallas kernels  40.3 us (97%)
  local copies, waits for them, and re-layouts  0.97 us (2%)
    pallas_call x1, Pallas kernels, shards(): pl.pallas_call(functools.partial(kernel, n_lat, n_lev, x_size, lev_total)...  40.3 us
    unnamed x1, local copies, waits for them, and re-layouts  0.97 us

profile of v4, /device:TPU:1, one launch (start us, length us, event | category | flops | bytes accessed | tf_op | source)
XLA Modules:
  0.0 41.3 jit_solution(10762391614151598643)
XLA Ops:
  0.0 40.3 %shard_map.82 = bf16[4,128,8,128]{3,2,1,0:T(8,128)(2,1)S(1)} custom-call(s32[1,32]{1,0:T(1,128)} %cnt_hbm.1, s32[6,16]{1,0:T(8,128)} %bitcast.5, f32[128,1152]{1,0:T(8,128)} %bitcast.3, f32[64,1152]{1,0:T(8,128)} %bitcast.4, bf16[128,128]{1,0:T(8,128)(2,1)} %rw_hbm.1, bf16[512,512]{1,0:T(8,128)(2,1)} %w1_hbm.1, bf16[512,512]{1,0:T(8,128)(2,1)} %w2_hbm.1, ...), custom_call_target="tpu_custom_call" | custom-call | tf_op jit(solution)/shard_map/pallas_call | solution.py:416
  40.3 1.0 %copy.10 = bf16[4,128,8,128]{3,2,1,0:T(8,128)(2,1)} copy(bf16[4,128,8,128]{3,2,1,0:T(8,128)(2,1)S(1)} %shard_map.82) | data formatting | bytes 2097152

commit v5 on v3

--- a/solution.py
+++ b/solution.py
@@ -40,29 +40,8 @@
     z_size = n_lev // x_size
     my_z, my_x = me // x_size, lax.rem(me, x_size)
     reach = z_size // 2 - 1
-    below, above = lax.rem(my_z + z_size - 1, z_size), lax.rem(my_z + 1, z_size)
-
-    def place(z, x):
-        return lax.rem(z, z_size) * x_size + lax.rem(x, x_size)
-
-    barrier = pltpu.get_barrier_semaphore()
-
-    def greet(where):
-        pl.semaphore_signal(barrier, inc=1, device_id=where, device_id_type=MESH)
-
-    for other in (up, down):
-        greet({"lat": other})
-
-    @pl.loop(0, reach * x_size)
-    def _(i):
-        greet({"lev": place(my_z + 1 + i // x_size, i)})
-        greet({"lev": place(my_z + z_size - 1 - i // x_size, i)})
-
-    @pl.loop(1, x_size)
-    def _(i):
-        greet({"lev": place(my_z, my_x + i)})
-
-    greeted = 2 + 2 * reach * x_size + x_size - 1
+    plane_at = {d: lax.rem(my_z + z_size + d, z_size) * x_size for d in range(-reach, reach + 1)}
+    x_at = [lax.rem(my_x + i, x_size) for i in range(x_size)]
 
     tiles = lon // SLOT
     columns = [slice(t * SLOT, (t + 1) * SLOT) for t in range(tiles)]
@@ -73,6 +52,26 @@
         inputs.append(pltpu.make_async_copy(winds_hbm.at[:, cut], wind_in.at[t], in_sem.at[1, t]))
     for copy in inputs:
         copy.start()
+
+    barrier = pltpu.get_barrier_semaphore()
+
+    def greet(where):
+        pl.semaphore_signal(barrier, inc=1, device_id=where, device_id_type=MESH)
+
+    for other in (up, down):
+        greet({"lat": other})
+
+    for d in range(1, reach + 1):
+
+        @pl.loop(0, x_size)
+        def _(x, d=d):
+            greet({"lev": plane_at[d] + x})
+            greet({"lev": plane_at[-d] + x})
+
+    for x in x_at[1:]:
+        greet({"lev": plane_at[0] + x})
+
+    greeted = 2 + 2 * reach * x_size + x_size - 1
 
     loads = [
         pltpu.make_async_copy(src, dst, load_sem.at[i])
@@ -173,68 +172,69 @@
 
     lane = lax.broadcasted_iota(jnp.int32, (group, SLOT), 1)
     last_bit = (tiles - 1).bit_length() - 1
-    to_right = [reach + 1 if c % 2 == 0 else reach for c in range(len(chunks))]
-
-    def first_slot(c, way):
-        return (0, x_size, x_size * (1 + to_right[c]))[way]
-
-    def planes(c, way):
-        return (1, to_right[c], 2 * reach + 1 - to_right[c])[way]
+    half = x_size // 2
+
+    def first_slot(way):
+        return (0, x_size, x_size * (1 + reach) + half)[way]
+
+    def planes(way):
+        return (1, reach + 1, reach + 1)[way]
+
+    def chips(way, j):
+        if j < reach:
+            return range(x_size)
+        return range(half) if way == 1 else range(half, x_size)
+
+    def slot(way, j, x):
+        return first_slot(way) + j * x_size + x - (half if way == 2 and j == reach else 0)
 
     def plane_of(way, j):
-        return my_z + z_size - j if way == 2 else my_z + j
+        return plane_at[-j if way == 2 else j]
 
     def source_of(way):
-        return (me, below * x_size + my_x, above * x_size + my_x)[way]
+        return plane_at[(0, -1, 1)[way]] + my_x
 
     def pack(c, way):
-        base = first_slot(c, way)
-
-        def body(i, carry):
-            start = starts[0, place(plane_of(way, i // x_size), i)]
-            tile = start >> 7
-            after = (tile + 1) - (tile >> last_bit)
-            shift = start & (SLOT - 1)
-            back = (SLOT - shift) & (SLOT - 1)
-            take = lane < SLOT - shift
-            for k in range(2):
-                if way == 0:
-                    a, b = raw_out[c, tile, k], raw_out[c, after, k]
-                else:
-                    arrived = raw_in[2 * c + way - 1]
-                    a, b = arrived[tile, k], arrived[after, k]
-                a, b = pltpu.roll(a, back, axis=1), pltpu.roll(b, back, axis=1)
-                send[c, base + i, :, k * SLOT : (k + 1) * SLOT] = jnp.where(take, a, b)
-            return carry
-
-        count = planes(c, way) * x_size
-        lax.fori_loop(0, count, body, 0, unroll=4 if count % 4 == 0 else 1)
+        for j in range(planes(way)):
+            owners = plane_of(way, j)
+            for x in chips(way, j):
+                start = starts[0, owners + x]
+                tile = start >> 7
+                after = (tile + 1) - (tile >> last_bit)
+                shift = start & (SLOT - 1)
+                back = (SLOT - shift) & (SLOT - 1)
+                take = lane < SLOT - shift
+                for k in range(2):
+                    if way == 0:
+                        a, b = raw_out[c, tile, k], raw_out[c, after, k]
+                    else:
+                        arrived = raw_in[2 * c + way - 1]
+                        a, b = arrived[tile, k], arrived[after, k]
+                    a, b = pltpu.roll(a, back, axis=1), pltpu.roll(b, back, axis=1)
+                    send[c, slot(way, j, x), :, k * SLOT : (k + 1) * SLOT] = jnp.where(take, a, b)
 
     def slot_copy(c, way, j, x):
-        source = source_of(way)
-        x = lax.rem(x, x_size)
         return pltpu.make_async_remote_copy(
-            src_ref=send.at[c, first_slot(c, way) + j * x_size + x],
-            dst_ref=recv.at[c, source],
+            src_ref=send.at[c, slot(way, j, x)],
+            dst_ref=recv.at[c, source_of(way)],
             send_sem=send_sem.at[c],
             recv_sem=recv_sem.at[c],
-            device_id={"lev": place(plane_of(way, j), x)},
+            device_id={"lev": plane_of(way, j) + x},
             device_id_type=MESH,
         )
 
     def ship(c, way):
-        far = planes(c, way) - 1
-        if far > 0:
-
-            @pl.loop(0, far * x_size)
-            def _(i):
-                slot_copy(c, way, far - i // x_size, i).start()
-
-        @pl.loop(1, x_size)
-        def _(i):
-            slot_copy(c, way, 0, my_x + i).start()
-
-        mine = send.at[c, first_slot(c, way) + my_x]
+        for j in range(planes(way) - 1, 0, -1):
+            span = chips(way, j)
+
+            @pl.loop(span[0], span[-1] + 1)
+            def _(x, j=j):
+                slot_copy(c, way, j, x).start()
+
+        for x in x_at[1:]:
+            slot_copy(c, way, 0, x).start()
+
+        mine = send.at[c, first_slot(way) + my_x]
         pltpu.make_async_copy(mine, recv.at[c, source_of(way)], recv_sem.at[c]).start()
 
     def raw_copy(c, w):
@@ -243,7 +243,7 @@
             dst_ref=raw_in[2 * c + w],
             send_sem=raw_send.at[w, c],
             recv_sem=raw_recv.at[w, c],
-            device_id={"lev": (above, below)[w] * x_size + my_x},
+            device_id={"lev": plane_at[(1, -1)[w]] + my_x},
             device_id_type=MESH,
         )
 
@@ -261,19 +261,12 @@
         pack(c, 0)
         ship(c, 0)
 
-    for r in range(rows):
+    for r in range(1, 5):
         make_side(r)
-    for j in range(1, rows):
+    for j in range(1, 6):
         make_face(j)
-    sweep(value, range(1, 7), first_step)
-    sweep(guess, range(2, 6), second_step)
-    loads[0].wait()
-
-    def prefix(k, start):
-        starts[0, k] = start
-        return start + cnt_ref[0, k]
-
-    lax.fori_loop(0, n_lev, prefix, jnp.int32(0))
+    sweep(value, range(1, 5), first_step)
+    sweep(guess, (2, 3), second_step)
 
     pl.semaphore_wait(barrier, greeted)
 
@@ -291,7 +284,22 @@
     for halo in halos:
         halo.start()
     send_raw(0)
+    for r in (5, 6):
+        make_side(r)
+    for j in (6, 7):
+        make_face(j)
+    sweep(value, (5, 6), first_step)
+    sweep(guess, (4, 5), second_step)
     send_raw(1)
+    for r in (0, 7):
+        make_side(r)
+    loads[0].wait()
+
+    def prefix(k, start):
+        starts[0, k] = start
+        return start + cnt_ref[0, k]
+
+    lax.fori_loop(0, n_lev, prefix, jnp.int32(0))
     own(0)
     own(1)
     relay(0)
@@ -312,6 +320,9 @@
     own(3)
     relay(1)
 
+    relay(2)
+    relay(3)
+
     def iota(shape, dim):
         return lax.broadcasted_iota(jnp.int32, shape, dim)
 
@@ -339,11 +350,9 @@
     w2t[...] = w2_in[...].astype(F32).T.astype(BF)
     w3t[...] = dot(order, w3_in[...].astype(F32).T.astype(BF)).astype(BF)
 
-    relay(2)
-    relay(3)
-
     def silu(x):
-        return x / (1.0 + jnp.exp(-x))
+        half = 0.5 * x
+        return half + half * jnp.tanh(half)
 
     for c, pair in enumerate(chunks):
         pltpu.make_async_copy(recv.at[c], recv.at[c], recv_sem.at[c]).wait()
@@ -357,13 +366,17 @@
             part = slice(i * SLOT, (i + 1) * SLOT)
             done[pl.ds(r, feats, stride=rows), :] = remapped[:, part] + hit * tendency[:, part]
 
-    keep = lane[:8] < cnt_ref[0, me]
-
-    @pl.loop(0, n_lev)
-    def _(src):
-        for q in range(group):
-            tile = done[pl.ds(pl.multiple_of((src * group + q) * rows, rows), rows), :]
-            out_ref[q // levels, src * levels + q % levels] = jnp.where(keep, tile, 0.0).astype(BF)
+    span = levels * rows
+    keep = lax.broadcasted_iota(jnp.int32, (span, SLOT), 1) < cnt_ref[0, me]
+
+    def finish(src, carry):
+        for f in range(fields_count):
+            part = done[pl.ds(pl.multiple_of((src * fields_count + f) * span, span), span), :]
+            where = pl.multiple_of((f * n_lev + src) * span, span)
+            out_ref[pl.ds(where, span), :] = jnp.where(keep, part, 0.0).astype(BF)
+        return carry
+
+    lax.fori_loop(0, n_lev, finish, 0, unroll=4)
 
     for c in range(len(chunks)):
         sent = send.at[c, pl.ds(0, n_lev - 3)]
@@ -386,7 +399,7 @@
     halo = (2 * halves + 2,) + plane
     return pl.pallas_call(
         functools.partial(kernel, n_lat, n_lev, x_size, lev_total),
-        out_shape=jax.ShapeDtypeStruct((field_count, lev_total, rows, SLOT), BF),
+        out_shape=jax.ShapeDtypeStruct((field_count * lev_total * rows, SLOT), BF),
         in_specs=[hbm, hbm, hbm, hbm, hbm, hbm, hbm, hbm],
         out_specs=vmem,
         scratch_shapes=[
@@ -421,7 +434,7 @@
     )(*(pltpu.with_memory_space_constraint(x, pltpu.HBM) for x in (
         lon_counts, group_list, fields.reshape(group * rows, lon), winds.reshape(2 * levels * rows, lon),
         remap_weight, w_first, w_second, w_third,
-    )))
+    ))).reshape(field_count, lev_total, rows, SLOT)
 
 
 def solution(mesh):

time: 39 us -> 37.9 us (0.972)
  the two profiles are of different devices: /device:TPU:1 before, /device:TPU:25 now
where the time goes in v5:
time: 37.9 us; the launch traced here: 37.7 us
  Pallas kernels  36.7 us (97%)
  local copies, waits for them, and re-layouts  0.97 us (3%)
    pallas_call x1, Pallas kernels, shards(): pl.pallas_call(functools.partial(kernel, n_lat, n_lev, x_size, lev_total)...  36.7 us
    unnamed x1, local copies, waits for them, and re-layouts  0.97 us

profile of v5, /device:TPU:25, one launch (start us, length us, event | category | flops | bytes accessed | tf_op | source)
XLA Modules:
  0.0 37.7 jit_solution(6175737645721459436)
XLA Ops:
  0.0 36.7 %shard_map.82 = bf16[4096,128]{1,0:T(8,128)(2,1)S(1)} custom-call(s32[1,32]{1,0:T(1,128)} %cnt_hbm.1, s32[6,16]{1,0:T(8,128)} %bitcast.7, f32[128,1152]{1,0:T(8,128)} %bitcast.5, f32[64,1152]{1,0:T(8,128)} %bitcast.6, bf16[128,128]{1,0:T(8,128)(2,1)} %rw_hbm.1, bf16[512,512]{1,0:T(8,128)(2,1)} %w1_hbm.1, bf16[512,512]{1,0:T(8,128)(2,1)} %w2_hbm.1, ...), custom_call_target="tpu_custom_call" | custom-call | tf_op jit(solution)/shard_map/pallas_call | solution.py:400
  36.7 1.0 %copy.10 = bf16[4,128,8,128]{3,2,1,0:T(8,128)(2,1)} copy(bf16[4,128,8,128]{3,2,1,0:T(8,128)(2,1)S(1)} %bitcast.4) | data formatting | bytes 2097152

commit v6 on v5

--- a/solution.py
+++ b/solution.py
@@ -10,6 +10,8 @@
 DIFFUSION = 0.15
 SLOT = 128
 X_SIZE = 4
+URGENT_FROM = 0
+LOW = 2
 LIMIT = 48000000
 MESH = pl.DeviceIdType.MESH
 BF = jnp.bfloat16
@@ -223,16 +225,28 @@
             device_id_type=MESH,
         )
 
+    def ship_plane(c, way, j):
+        span = chips(way, j)
+        if j > 0:
+
+            @pl.loop(span[0], span[-1] + 1)
+            def _(x):
+                slot_copy(c, way, j, x).start()
+
+        else:
+            for x in x_at[1:]:
+                slot_copy(c, way, 0, x).start()
+
     def ship(c, way):
-        for j in range(planes(way) - 1, 0, -1):
-            span = chips(way, j)
-
-            @pl.loop(span[0], span[-1] + 1)
-            def _(x, j=j):
-                slot_copy(c, way, j, x).start()
-
-        for x in x_at[1:]:
-            slot_copy(c, way, 0, x).start()
+        order = range(planes(way) - 1, -1, -1)
+        if c < URGENT_FROM or way == 0:
+            for j in order:
+                ship_plane(c, way, j)
+        else:
+            for first in (True, False):
+                for j in order:
+                    low = plane_of(way, j) < LOW * x_size
+                    pl.when(low if first else jnp.logical_not(low))(functools.partial(ship_plane, c, way, j))
 
         mine = send.at[c, first_slot(way) + my_x]
         pltpu.make_async_copy(mine, recv.at[c, source_of(way)], recv_sem.at[c]).start()

time: 37.9 us -> 37.6 us (level)
  the two profiles are of different devices: /device:TPU:25 before, /device:TPU:6 now
where the time goes in v6:
time: 37.6 us; the launch traced here: 37.5 us
  Pallas kernels  36.5 us (97%)
  local copies, waits for them, and re-layouts  0.97 us (3%)
    pallas_call x1, Pallas kernels, shards(): pl.pallas_call(functools.partial(kernel, n_lat, n_lev, x_size, lev_total)...  36.5 us
    unnamed x1, local copies, waits for them, and re-layouts  0.97 us

profile of v6, /device:TPU:6, one launch (start us, length us, event | category | flops | bytes accessed | tf_op | source)
XLA Modules:
  0.0 37.5 jit_solution(13115853980315650723)
XLA Ops:
  0.0 36.5 %shard_map.82 = bf16[4096,128]{1,0:T(8,128)(2,1)S(1)} custom-call(s32[1,32]{1,0:T(1,128)} %cnt_hbm.1, s32[6,16]{1,0:T(8,128)} %bitcast.7, f32[128,1152]{1,0:T(8,128)} %bitcast.5, f32[64,1152]{1,0:T(8,128)} %bitcast.6, bf16[128,128]{1,0:T(8,128)(2,1)} %rw_hbm.1, bf16[512,512]{1,0:T(8,128)(2,1)} %w1_hbm.1, bf16[512,512]{1,0:T(8,128)(2,1)} %w2_hbm.1, ...), custom_call_target="tpu_custom_call" | custom-call | tf_op jit(solution)/shard_map/pallas_call | solution.py:414
  36.5 1.0 %copy.10 = bf16[4,128,8,128]{3,2,1,0:T(8,128)(2,1)} copy(bf16[4,128,8,128]{3,2,1,0:T(8,128)(2,1)S(1)} %bitcast.4) | data formatting | bytes 2097152

commit v7 on v6

--- a/solution.py
+++ b/solution.py
@@ -295,9 +295,9 @@
         )
         for i, (src, dst, other) in enumerate(((up_buf, lo_buf, up), (down_buf, hi_buf, down)))
     ]
+    send_raw(0)
     for halo in halos:
         halo.start()
-    send_raw(0)
     for r in (5, 6):
         make_side(r)
     for j in (6, 7):

time: 37.6 us -> 37.6 us (level)
  no operation moved by 1% of the time
where the time goes in v7:
time: 37.6 us; the launch traced here: 37.5 us
  Pallas kernels  36.5 us (97%)
  local copies, waits for them, and re-layouts  0.97 us (3%)
    pallas_call x1, Pallas kernels, shards(): pl.pallas_call(functools.partial(kernel, n_lat, n_lev, x_size, lev_total)...  36.5 us
    unnamed x1, local copies, waits for them, and re-layouts  0.97 us

profile of v7, /device:TPU:6, one launch (start us, length us, event | category | flops | bytes accessed | tf_op | source)
XLA Modules:
  0.0 37.5 jit_solution(14376492575179804906)
XLA Ops:
  0.0 36.5 %shard_map.82 = bf16[4096,128]{1,0:T(8,128)(2,1)S(1)} custom-call(s32[1,32]{1,0:T(1,128)} %cnt_hbm.1, s32[6,16]{1,0:T(8,128)} %bitcast.7, f32[128,1152]{1,0:T(8,128)} %bitcast.5, f32[64,1152]{1,0:T(8,128)} %bitcast.6, bf16[128,128]{1,0:T(8,128)(2,1)} %rw_hbm.1, bf16[512,512]{1,0:T(8,128)(2,1)} %w1_hbm.1, bf16[512,512]{1,0:T(8,128)(2,1)} %w2_hbm.1, ...), custom_call_target="tpu_custom_call" | custom-call | tf_op jit(solution)/shard_map/pallas_call | solution.py:414
  36.5 1.0 %copy.10 = bf16[4,128,8,128]{3,2,1,0:T(8,128)(2,1)} copy(bf16[4,128,8,128]{3,2,1,0:T(8,128)(2,1)S(1)} %bitcast.4) | data formatting | bytes 2097152
